TPU v7x, 32 devices: a whole 2x2x4 slice. The times are simulated.
32 devices in a mesh: groups: 2 (over x), gx: 4 (over y, core), gy: 4 (over z).
Axes of the slice: x: 2, y: 2, z: 4, core: 2. Of those that a mesh axis runs over, the one named last changes fastest.
Arguments:
- tokens: bfloat16 [64, 2, 16384], P('groups', None, 'gx'), parts along dimension 0
- norm_gain: bfloat16 [16384], P('gx'), may hold values from 0.099609375 to 1.8984375
- qkv_weight: bfloat16 [16384, 8, 18, 128], P('gx', 'gy'), may hold values from -0.046875 to 0.046875
- out_weight: bfloat16 [128, 128, 16384], P('gy', None, 'gx'), may hold values from -0.125 to 0.125
- kv_cache: bfloat16 [64, 384, 2, 8, 128], P(('groups', 'gx', 'gy')), parts along dimension 0
- lengths: int32 [64], P(('groups', 'gx', 'gy')), parts along dimension 0, may hold values from 1 to 384, as said below
- positions: int32 [64], P('groups'), parts along dimension 0, may hold values from 0 to 4095
Outputs:
- layer_out: float32 [64, 2, 16384], P(('groups', 'gy'), None, 'gx'), parts along dimension 0
There are 2 independent parts, one for each index of `groups`. A program takes and returns all parts, laid end to end along the dimension named above; an argument that names none is the same for every part. Nothing has to cross between parts.
Inputs may be any that keep to these rules, and one draw needn't show every extreme that they name: Cache slots 0 to lengths - 1 of a row hold its earlier tokens; some row has exactly 384.
All inputs are finite; a program needn't handle non-finite values.
Results may differ from a plain program's by a relative error of at most 0.025.
Values may be sent and summed in bfloat16 or wider, within the bound.
A program may use at most 192 MiB of HBM per device.

v0:
```python
import math

import jax
import jax.numpy as jnp
from jax import lax
from jax.sharding import PartitionSpec as P

D = 16384


norm_eps = 1e-05
rope_base = 500000.0


def rotate(values, places):
    half_dim = values.shape[-1] // 2
    index_half = jnp.arange(half_dim, dtype=jnp.float32)
    frequency = rope_base ** (-2.0 * index_half / values.shape[-1])
    angles = places[..., None] * frequency
    cosine = jnp.cos(angles)
    sine_part = jnp.sin(angles)
    front_half = values[..., :half_dim]
    back_half = values[..., half_dim:]
    return jnp.concatenate(
        [front_half * cosine - back_half * sine_part, back_half * cosine + front_half * sine_part],
        axis=-1,
    )


def finish(projected, positions, first_row, row_count):
    group_size = projected.shape[3] - 2
    placed = lax.dynamic_slice_in_dim(positions, first_row, row_count, 0)
    places = (placed[:, None] + jnp.arange(2, dtype=jnp.int32)[None, :]).astype(jnp.float32)
    queries = rotate(projected[:, :, :, :group_size], places[:, :, None, None])
    key_new = rotate(projected[:, :, :, group_size : group_size + 1], places[:, :, None, None])
    value_new = projected[:, :, :, group_size + 1 :]
    return jnp.concatenate([queries, key_new, value_new], axis=3).astype(jnp.bfloat16)


def attend(queries, key_new, value_new, cache_rows, length):
    scale_factor = 1.0 / math.sqrt(queries.shape[-1])
    scores_old = (
        jnp.einsum(
            "rtgid,rsgd->rtgis", queries, cache_rows[:, :, 0], preferred_element_type=jnp.float32
        )
        * scale_factor
    )
    slot_ids = jnp.arange(cache_rows.shape[1], dtype=jnp.int32)
    visible = slot_ids[None, :] < length[:, None]
    scores_old = jnp.where(visible[:, None, None, None, :], scores_old, -1e30)
    scores_new = (
        jnp.einsum("rtgid,rugd->rtgiu", queries, key_new, preferred_element_type=jnp.float32)
        * scale_factor
    )
    token_ids = jnp.arange(queries.shape[1], dtype=jnp.int32)
    causal = token_ids[:, None] >= token_ids[None, :]
    scores_new = jnp.where(causal[None, :, None, None, :], scores_new, -1e30)
    highest = jnp.maximum(jnp.max(scores_old, axis=-1), jnp.max(scores_new, axis=-1))
    expo_old = jnp.exp(scores_old - highest[..., None])
    expo_new = jnp.exp(scores_new - highest[..., None])
    denominator = jnp.sum(expo_old, axis=-1) + jnp.sum(expo_new, axis=-1)
    weight_old = (expo_old / denominator[..., None]).astype(jnp.bfloat16)
    weight_new = (expo_new / denominator[..., None]).astype(jnp.bfloat16)
    attended = jnp.einsum(
        "rtgis,rsgd->rtgid", weight_old, cache_rows[:, :, 1], preferred_element_type=jnp.float32
    )
    attended = attended + jnp.einsum(
        "rtgiu,rugd->rtgid", weight_new, value_new, preferred_element_type=jnp.float32
    )
    return attended.astype(jnp.bfloat16)


def body(tokens, norm_gain, qkv_weight, out_weight, kv_cache, lengths, positions):
    rows_local = kv_cache.shape[0]
    head_devices = lax.axis_size("gy")
    width_index = lax.axis_index("gx")
    head_index = lax.axis_index("gy")
    total_rows = tokens.shape[0]
    local_width = tokens.shape[2]
    groups_local = qkv_weight.shape[1]
    group_width = qkv_weight.shape[2]
    head_dim = qkv_weight.shape[3]
    group_size = group_width - 2
    tokens_wide = tokens.astype(jnp.float32)
    hidden = (tokens_wide * norm_gain.astype(jnp.float32)).astype(jnp.bfloat16)
    squares = jnp.sum(tokens_wide * tokens_wide, axis=-1)
    block_rows = rows_local * head_devices
    partial_value = jnp.dot(
        hidden.reshape(total_rows * 2, local_width),
        qkv_weight.reshape(local_width, -1),
        preferred_element_type=jnp.float32,
    )
    partial_value = partial_value.reshape(total_rows, 2, groups_local, group_width, head_dim)
    block_sum, block_squares = (
        lax.psum_scatter(partial_value, "gx", scatter_dimension=0, tiled=True),
        lax.psum_scatter(squares, "gx", scatter_dimension=0, tiled=True),
    )
    inv_rms = lax.rsqrt(block_squares / D + norm_eps)
    ready = finish(
        block_sum * inv_rms[:, :, None, None, None], positions, width_index * block_rows, block_rows
    )
    packed = lax.all_to_all(ready, "gy", split_axis=0, concat_axis=2, tiled=True)
    queries = packed[:, :, :, :group_size]
    key_new = packed[:, :, :, group_size]
    value_new = packed[:, :, :, group_size + 1]
    attended = attend(queries, key_new, value_new, kv_cache, lengths)
    regrouped = lax.all_to_all(attended, "gy", split_axis=2, concat_axis=0, tiled=True)
    out_flat = out_weight.reshape(-1, local_width)
    row_piece = lax.all_gather(regrouped, "gx", axis=0, tiled=True)
    piece_rows = row_piece.shape[0]
    product = jnp.dot(
        row_piece.reshape(piece_rows * 2, -1), out_flat, preferred_element_type=jnp.float32
    )
    terms = product.reshape(piece_rows, 2, local_width)
    own_sum = lax.psum_scatter(terms, "gy", scatter_dimension=0, tiled=True)
    row_share = total_rows // head_devices
    residual = lax.dynamic_slice_in_dim(tokens, head_index * row_share, row_share, 0).astype(
        jnp.float32
    )
    return residual + own_sum


def solution(mesh):
    return jax.shard_map(
        body,
        mesh=mesh,
        in_specs=(
            P("groups", None, "gx"),
            P("gx"),
            P("gx", "gy", None, None),
            P("gy", None, "gx"),
            P(("groups", "gx", "gy"), None, None, None, None),
            P(("groups", "gx", "gy")),
            P("groups"),
        ),
        out_specs=P(("groups", "gy"), None, "gx"),
        check_vma=False,
    )
```

profile of v0, /device:TPU:0, one launch (start us, length us, event | category | flops | bytes accessed | tf_op | source)
XLA Modules:
  0.0 225.1 jit_solution(11655905521266195650)
XLA Ops:
  6.5 0.0 copy-start.1
  6.5 0.0 copy-start
  6.5 0.0 reduce-scatter.4.cloned.1.call-start
  6.5 91.1 %copy.60 = bf16[4096,2,18,128]{0,3,2,1:T(8,128)(2,1)} copy(bf16[4096,2,18,128]{3,1,2,0:T(2,128)(2,1)} %param.9) | data formatting | bytes 75497472 | tf_op args[2]
  97.7 0.0 copy-done.1
  97.7 0.0 copy-done
  97.7 1.1 fusion.13
  98.8 0.0 copy-start.4
  98.8 0.0 copy-start.3
  98.8 17.5 %fusion = f32[32,2,2,18,128]{4,0,3,2,1:T(8,128)} fusion(bf16[4096,2,18,128]{0,3,2,1:T(8,128)(2,1)} %copy.60, bf16[32,2,4096,1,1]{2,1,0,4,3:T(2,128)(2,1)S(1)} %get-tuple-element.8), kind=kOutput, calls=%fused_computation | convolution fusion | flops 2415919104 | bytes 39452672 | tf_op jit(solution)/shard_map/dot_general | solution.py:88
  116.3 0.0 reduce-scatter.4.cloned.1.call-update
  116.3 0.1 copy.62
  116.4 0.0 copy-done.4
  116.4 0.6 dynamic-slice
  117.7 0.0 copy-done.3
  117.7 0.1 dynamic_slice.7
  117.7 8.4 %all-reduce = f32[32,2]{0,1:T(2,128)S(1)} all-reduce(f32[32,2]{0,1:T(2,128)S(1)} %copy.62), channel_id=3, replica_groups=mesh['groups'=2,'gx'=4,'gy'=4] {'gx'}, use_global_device_ids=true, to_apply=%region_2.0.clone | all-reduce | flops 64 | bytes 512
  126.1 0.1 fusion.29
  126.2 0.1 multiply_cosine_fusion
  126.3 2.2 fusion.30
  128.6 0.0 copy-start.2
  128.6 16.2 %reduce-scatter.4.cloned.1.call-done = f32[8,2,2,18,128]{4,0,3,2,1:T(8,128)} async-done(((f32[32,2,2,18,128]{4,0,3,2,1:T(8,128)}), f32[8,2,2,18,128]{4,0,3,2,1:T(8,128)}) %reduce-scatter.4.cloned.1.call-update) | async-done | bytes 294928 | tf_op jit(solution)/shard_map/reduce_scatter | solution.py:95
  144.8 1.0 broadcast_multiply_fusion
  145.9 0.1 subtract_convert_fusion.1
  145.9 0.1 subtract_convert_fusion
  146.1 0.1 pad_maximum_fusion
  146.2 0.8 copy.63
  147.0 4.6 %all-to-all-start = ((bf16[8,2,2,18,128]{4,2,3,1,0:T(2,128)(2,1)}), bf16[8,2,2,18,128]{4,2,3,1,0:T(2,128)(2,1)S(1)}, u32[]{:S(2)}, u32[]{:S(2)}) async-start(bf16[8,2,2,18,128]{4,2,3,1,0:T(2,128)(2,1)} %copy.63), calls=%async_computation.1 | async-start | bytes 294912 | tf_op jit(solution)/shard_map/all_to_all | solution.py:102
  151.6 0.0 reduce-scatter.6.cloned.1.call-start
  151.6 0.0 copy-done.2
  151.6 0.1 iota_compare_fusion
  151.7 6.2 %all-to-all-done = bf16[8,2,2,18,128]{4,2,3,1,0:T(2,128)(2,1)S(1)} async-done(((bf16[8,2,2,18,128]{4,2,3,1,0:T(2,128)(2,1)}), bf16[8,2,2,18,128]{4,2,3,1,0:T(2,128)(2,1)S(1)}, u32[]{:S(2)}, u32[]{:S(2)}) %all-to-all-start) | async-done | bytes 147488 | tf_op jit(solution)/shard_map/all_to_all | solution.py:102
  157.9 0.4 fusion.33
  158.4 0.8 fusion.32
  159.2 0.3 fusion.14
  159.5 0.1 fusion.23
  159.6 0.2 convolution_bitcast_fusion
  159.8 0.5 fusion.9
  160.4 8.4 %all_to_all.36 = bf16[2,2,8,16,128]{4,3,1,0,2:T(8,128)(2,1)S(1)} all-to-all(bf16[2,2,8,16,128]{4,3,1,0,2:T(8,128)(2,1)S(1)} %copy.71), channel_id=1, replica_groups=mesh['groups'=2,'gx'=4,'gy'=4] {'gy'}, dimensions={2} | all-to-all | bytes 262144 | tf_op jit(solution)/shard_map/all_to_all | solution.py:107
  168.8 6.5 %all_gather.3 = bf16[32,2,2,16,128]{4,3,2,1,0:T(8,128)(2,1)S(1)} all-gather(bf16[8,2,2,16,128]{4,3,2,1,0:T(8,128)(2,1)S(1)} %bitcast.81), channel_id=1, replica_groups=mesh['groups'=2,'gx'=4,'gy'=4] {'gx'}, dimensions={0}, use_global_device_ids=true | all-gather | bytes 655360 | tf_op jit(solution)/shard_map/all_gather | solution.py:109
  175.4 0.1 reshape.103
  175.5 14.6 %fusion.16 = f32[32,2,4096]{2,0,1:T(8,128)} fusion(bf16[4096,4096,1]{1,0,2:T(8,128)(2,1)} %bitcast.76, bf16[32,2,4096]{2,1,0:T(2,128)(2,1)S(1)} %reshape.103), kind=kOutput, calls=%fused_computation.24 | convolution fusion | flops 2147483648 | bytes 35127296 | tf_op jit(solution)/shard_map/dot_general | solution.py:111
  190.1 0.0 reduce-scatter.6.cloned.1.call-update
  190.1 1.0 constant_dynamic-slice_fusion
  191.1 25.1 %reduce-scatter.6.cloned.1.call-done = f32[8,2,4096]{2,0,1:T(8,128)} async-done(((f32[32,2,4096]{2,0,1:T(8,128)}), f32[8,2,4096]{2,0,1:T(8,128)}) %reduce-scatter.6.cloned.1.call-update) | async-done | bytes 262160 | tf_op jit(solution)/shard_map/reduce_scatter | solution.py:115
  216.3 1.0 convert_add_fusion
  217.3 0.9 copy.75
  (12 shorter events, 0.1 us)
Async XLA Ops:
  6.5 91.1 %copy-start.1 = (bf16[4096]{0:T(1024)(128)(2,1)S(1)}, bf16[4096]{0:T(1024)(128)(2,1)}, u32[]{:S(2)}) copy-start(bf16[4096]{0:T(1024)(128)(2,1)} %param.8) | copy-start | bytes 24580
  6.5 91.1 %copy-start = (bf16[32,2,4096]{2,1,0:T(2,128)(2,1)S(1)}, bf16[32,2,4096]{2,1,0:T(2,128)(2,1)}, u32[]{:S(2)}) copy-start(bf16[32,2,4096]{2,1,0:T(2,128)(2,1)} %param.7) | copy-start | bytes 1572868
  6.5 138.3 %reduce-scatter.4.cloned.1.call-start = ((), (), s32[]{:S(2)}) async-start(), calls=%async_computation.4 | async-start | bytes 1474560 | tf_op jit(solution)/shard_map/reduce_scatter | solution.py:95
  98.8 17.7 %copy-start.4 = (u32[32]{0:T(128)S(1)}, u32[32]{0:T(128)}, u32[]{:S(2)}) copy-start(u32[32]{0:T(128)} %constant.39) | copy-start | bytes 388
  98.8 18.9 %copy-start.3 = (s32[32]{0:T(128)S(1)}, s32[32]{0:T(128)}, u32[]{:S(2)}) copy-start(s32[32]{0:T(128)} %param.13) | copy-start | bytes 388
  128.6 23.0 %copy-start.2 = (s32[2]{0:T(128)S(1)}, s32[2]{0:T(128)}, u32[]{:S(2)}) copy-start(s32[2]{0:T(128)} %param.12) | copy-start | bytes 28
  147.0 10.9 %all-to-all-start = ((bf16[8,2,2,18,128]{4,2,3,1,0:T(2,128)(2,1)}), bf16[8,2,2,18,128]{4,2,3,1,0:T(2,128)(2,1)S(1)}, u32[]{:S(2)}, u32[]{:S(2)}) async-start(bf16[8,2,2,18,128]{4,2,3,1,0:T(2,128)(2,1)} %copy.63), calls=%async_computation.1 | async-start | bytes 294912 | tf_op jit(solution)/shard_map/all_to_all | solution.py:102
  151.6 64.7 %reduce-scatter.6.cloned.1.call-start = ((), (), s32[]{:S(2)}) async-start(), calls=%async_computation.5 | async-start | bytes 1310720 | tf_op jit(solution)/shard_map/reduce_scatter | solution.py:115
Sparse Core Ops, SparseCore 0:
  116.4 28.3 reduce-scatter.3
  190.2 25.9 reduce-scatter.5
where the time goes:
time: 228 us; the launch traced here: 225 us
  local copies, waits for them, and re-layouts  97 us (43%)
  waiting for transfers between devices  47.6 us (21%)
  matrix products  34.1 us (15%)
  blocking collectives  23.3 us (10%)
  between operations  14.2 us (6%)
  starting transfers between devices  4.61 us (2%)
  other arithmetic  4.22 us (2%)
    unnamed x12, local copies, waits for them, and re-layouts  91.7 us
    reduce_scatter x1, waiting for transfers between devices, body(): own_sum = lax.psum_scatter(terms, 'gy', scatter_dimension=0, tiled=True)  25.1 us
    dot_general x1, matrix products, body(): jnp.dot(hidden.reshape(total_rows * 2, local_width), qkv_weight.reshape(l...  17.5 us
    reduce_scatter x1, waiting for transfers between devices, body(): lax.psum_scatter(partial_value, 'gx', scatter_dimension=0, tiled=True)  16.2 us
    dot_general x1, matrix products, body(): jnp.dot(row_piece.reshape(piece_rows * 2, -1), out_flat, preferred_elemen...  14.6 us
    all_to_all x1, blocking collectives, body(): lax.all_to_all(attended, 'gy', split_axis=2, concat_axis=0, tiled=True)  8.45 us
    unnamed x1, blocking collectives  8.37 us
    all_gather x1, blocking collectives, body(): row_piece = lax.all_gather(regrouped, 'gx', axis=0, tiled=True)  6.5 us
  transfers between devices with their start and end apart: 3, of which 3 were waited for; matrix products, arithmetic and copies ran while one was open for 2% of the time, Pallas kernels for 0%

commit v1 on v0

--- a/solution.py
+++ b/solution.py
@@ -1,8 +1,11 @@
+import functools
 import math
 
 import jax
 import jax.numpy as jnp
 from jax import lax
+from jax.experimental import pallas as pl
+from jax.experimental.pallas import tpu as pltpu
 from jax.sharding import PartitionSpec as P
 
 D = 16384
@@ -70,6 +73,124 @@
     return attended.astype(jnp.bfloat16)
 
 
+def project_kernel(
+    places, block_rows, steps, depth, tokens_ref, gain_ref, weight_ref, out_ref, held, total, squares, sems
+):
+    groups, columns, head_dim = 2, weight_ref.shape[1], weight_ref.shape[3]
+    slots = held.shape[0]
+    total_tokens = tokens_ref.shape[0]
+
+    def fetch(step, slot, column):
+        start = step * depth
+        if not isinstance(step, int):
+            start = pl.multiple_of(start, depth)
+        return pltpu.make_async_copy(
+            weight_ref.at[pl.ds(start, depth), column], held.at[slot, column], sems.at[slot, column]
+        )
+
+    for step in range(slots - 1):
+        for column in range(columns):
+            fetch(step, step, column).start()
+    total[...] = jnp.zeros_like(total)
+    squares[...] = jnp.zeros_like(squares)
+    feature = lax.broadcasted_iota(jnp.int32, (128, 256), 0)
+    target = lax.broadcasted_iota(jnp.int32, (128, 256), 1)
+    spreads = [
+        jnp.where(target == feature * groups + group, 1.0, 0.0).astype(jnp.bfloat16)
+        for group in range(groups)
+    ]
+
+    @pl.loop(0, steps)
+    def _(step):
+        slot = lax.rem(step, slots)
+
+        @pl.when(step + slots - 1 < steps)
+        def _():
+            later = step + slots - 1
+            for column in range(columns):
+                fetch(later, lax.rem(later, slots), column).start()
+
+        start = pl.multiple_of(step * depth, depth)
+        wide = tokens_ref[:, pl.ds(start, depth)].astype(jnp.float32)
+        squares[...] += sum(
+            wide[:, at : at + 128] * wide[:, at : at + 128] for at in range(0, depth, 128)
+        )
+        hidden = (wide * gain_ref[:, pl.ds(start, depth)].astype(jnp.float32)).astype(jnp.bfloat16)
+        parts = []
+        for at in range(0, depth, 128):
+            spread = [
+                jnp.dot(
+                    hidden[:, at : at + 128], spreads[group], preferred_element_type=jnp.float32
+                ).astype(jnp.bfloat16)
+                for group in range(groups)
+            ]
+            parts.append(
+                jnp.concatenate(
+                    [
+                        spread[group][row : row + block_rows]
+                        for row in range(0, total_tokens, block_rows)
+                        for group in range(groups)
+                    ],
+                    axis=0,
+                )
+            )
+        left = jnp.concatenate(parts, axis=1)
+        for column in range(0, columns, 2):
+            for near in (column, column + 1):
+                fetch(step, slot, near).wait()
+            right = jnp.concatenate(
+                [
+                    held.at[slot, near].reshape(depth * groups, head_dim)[...]
+                    for near in (column, column + 1)
+                ],
+                axis=1,
+            )
+            span = pl.ds(column * head_dim, 2 * head_dim)
+            total[:, span] += jnp.dot(left, right, preferred_element_type=jnp.float32)
+
+    width = columns * head_dim
+    out_ref[:, :width] = total[...].astype(jnp.bfloat16)
+    summed = jnp.sum(squares[...], axis=1, keepdims=True)
+    coarse = summed.astype(jnp.bfloat16).astype(jnp.float32)
+    lane = lax.broadcasted_iota(jnp.int32, (total_tokens, 128), 1)
+    extra = jnp.where(lane < 64, coarse, summed - coarse)
+    extra = jnp.concatenate(
+        [
+            extra[row : row + block_rows]
+            for row in range(0, total_tokens, block_rows)
+            for _ in range(groups)
+        ],
+        axis=0,
+    )
+    out_ref[:, width:] = extra.astype(jnp.bfloat16)
+
+
+def project(tokens, norm_gain, qkv_weight, places):
+    total_rows, pair, local_width = tokens.shape
+    groups, columns, head_dim = qkv_weight.shape[1:]
+    total_tokens = total_rows * pair
+    block_rows = total_tokens // places
+    depth, slots = 512, 3
+    steps = local_width // depth
+    view = jnp.transpose(qkv_weight, (0, 2, 1, 3))
+    vmem = pl.BlockSpec(memory_space=pltpu.VMEM)
+    return pl.pallas_call(
+        functools.partial(project_kernel, places, block_rows, steps, depth),
+        out_shape=jax.ShapeDtypeStruct(
+            (total_tokens * groups, (columns + 1) * head_dim), jnp.bfloat16
+        ),
+        in_specs=[vmem, vmem, pl.BlockSpec(memory_space=pl.ANY)],
+        out_specs=vmem,
+        scratch_shapes=[
+            pltpu.VMEM((slots, columns, depth, groups, head_dim), jnp.bfloat16),
+            pltpu.VMEM((total_tokens * groups, columns * head_dim), jnp.float32),
+            pltpu.VMEM((total_tokens, 128), jnp.float32),
+            pltpu.SemaphoreType.DMA((slots, columns)),
+        ],
+        compiler_params=pltpu.CompilerParams(vmem_limit_bytes=40 << 20),
+    )(tokens.reshape(total_tokens, local_width), norm_gain.reshape(1, local_width), view)
+
+
 def body(tokens, norm_gain, qkv_weight, out_weight, kv_cache, lengths, positions):
     rows_local = kv_cache.shape[0]
     head_devices = lax.axis_size("gy")
@@ -81,20 +202,30 @@
     group_width = qkv_weight.shape[2]
     head_dim = qkv_weight.shape[3]
     group_size = group_width - 2
-    tokens_wide = tokens.astype(jnp.float32)
-    hidden = (tokens_wide * norm_gain.astype(jnp.float32)).astype(jnp.bfloat16)
-    squares = jnp.sum(tokens_wide * tokens_wide, axis=-1)
     block_rows = rows_local * head_devices
-    partial_value = jnp.dot(
-        hidden.reshape(total_rows * 2, local_width),
-        qkv_weight.reshape(local_width, -1),
-        preferred_element_type=jnp.float32,
-    )
-    partial_value = partial_value.reshape(total_rows, 2, groups_local, group_width, head_dim)
-    block_sum, block_squares = (
-        lax.psum_scatter(partial_value, "gx", scatter_dimension=0, tiled=True),
-        lax.psum_scatter(squares, "gx", scatter_dimension=0, tiled=True),
-    )
+    places = lax.axis_size("gx")
+    if groups_local == 2 and group_width % 2 == 0 and local_width % 512 == 0:
+        partial_value = project(tokens, norm_gain, qkv_weight, places)
+        partial_value = partial_value.reshape(places, groups_local * block_rows * 2, -1)
+        pieces = lax.all_to_all(partial_value, "gx", split_axis=0, concat_axis=0)
+        summed = jnp.sum(pieces.astype(jnp.float32), axis=0)
+        summed = summed.reshape(groups_local, block_rows, 2, group_width + 1, head_dim)
+        block_squares = summed[0, :, :, group_width, 0] + summed[0, :, :, group_width, 64]
+        block_sum = jnp.transpose(summed[:, :, :, :group_width], (1, 2, 0, 3, 4))
+    else:
+        tokens_wide = tokens.astype(jnp.float32)
+        hidden = (tokens_wide * norm_gain.astype(jnp.float32)).astype(jnp.bfloat16)
+        squares = jnp.sum(tokens_wide * tokens_wide, axis=-1)
+        partial_value = jnp.dot(
+            hidden.reshape(total_rows * 2, local_width),
+            qkv_weight.reshape(local_width, -1),
+            preferred_element_type=jnp.float32,
+        )
+        partial_value = partial_value.reshape(total_rows, 2, groups_local, group_width, head_dim)
+        block_sum, block_squares = (
+            lax.psum_scatter(partial_value, "gx", scatter_dimension=0, tiled=True),
+            lax.psum_scatter(squares, "gx", scatter_dimension=0, tiled=True),
+        )
     inv_rms = lax.rsqrt(block_squares / D + norm_eps)
     ready = finish(
         block_sum * inv_rms[:, :, None, None, None], positions, width_index * block_rows, block_rows
@@ -111,8 +242,9 @@
     product = jnp.dot(
         row_piece.reshape(piece_rows * 2, -1), out_flat, preferred_element_type=jnp.float32
     )
-    terms = product.reshape(piece_rows, 2, local_width)
-    own_sum = lax.psum_scatter(terms, "gy", scatter_dimension=0, tiled=True)
+    terms = product.astype(jnp.bfloat16).reshape(head_devices, -1, 2, local_width)
+    arrived = lax.all_to_all(terms, "gy", split_axis=0, concat_axis=0)
+    own_sum = jnp.sum(arrived.astype(jnp.float32), axis=0)
     row_share = total_rows // head_devices
     residual = lax.dynamic_slice_in_dim(tokens, head_index * row_share, row_share, 0).astype(
         jnp.float32

time: 228 us -> 116 us (0.51); the launches traced: 225 us -> 116 us
  local copies, waits for them, and re-layouts: 97 us -> 8.24 us
  Pallas kernels: 0 us -> 32.1 us
  waiting for transfers between devices: 47.6 us -> 27.6 us
  matrix products: 34.1 us -> 15.6 us
  between operations: 14.2 us -> 0.21 us
  starting transfers between devices: 4.61 us -> 13.3 us
  blocking collectives: 23.3 us -> 14.8 us
    unnamed x12 -> x8, local copies, waits for them, and re-layouts: 91.7 us -> 0.47 us
    reduce_scatter x2 -> x0, waiting for transfers between devices: 41.4 us -> none  [the longest x1 25.1 us: body(): own_sum = lax.psum_scatter(terms, 'gy', scatter_dimension=0, tiled=True)]
    pallas_call x0 -> x1, Pallas kernels: none -> 32.1 us  [project(): pl.pallas_call(functools.partial(project_kernel, places, block_rows, step...]
    all_to_all x0 -> x2, waiting for transfers between devices: none -> 21.5 us  [the longest x1 15.2 us: body(): arrived = lax.all_to_all(terms, 'gy', split_axis=0, concat_axis=0)]
    dot_general x1 -> x0, matrix products: 17.5 us -> none  [body(): jnp.dot(hidden.reshape(total_rows * 2, local_width), qkv_weight.reshape(l...]
    unnamed x1 -> x0, blocking collectives: 8.37 us -> none
    all_to_all x0 -> x2, starting transfers between devices: none -> 7.74 us  [the longest x1 4.27 us: body(): pieces = lax.all_to_all(partial_value, 'gx', split_axis=0, concat_axis=0)]
    reshape x0 -> x5, local copies, waits for them, and re-layouts: none -> 3.34 us  [the longest x1 1.24 us: project(): tokens.reshape(total_tokens, local_width)]
  transfers between devices with their start and end apart: 3 -> 3, of which waited for: 3 -> 3; matrix products, arithmetic and copies ran while one was open for 2% -> 3% of each run, Pallas kernels for 0% -> 0%
where the time goes in v1:
time: 116 us
  Pallas kernels  32.1 us (28%)
  waiting for transfers between devices  27.6 us (24%)
  matrix products  15.6 us (13%)
  blocking collectives  14.8 us (13%)
  starting transfers between devices  13.3 us (11%)
  local copies, waits for them, and re-layouts  8.24 us (7%)
  other arithmetic  3.72 us (3%)
    pallas_call x1, Pallas kernels, project(): pl.pallas_call(functools.partial(project_kernel, places, block_rows, step...  32.1 us
    all_to_all x1, waiting for transfers between devices, body(): arrived = lax.all_to_all(terms, 'gy', split_axis=0, concat_axis=0)  15.2 us
    dot_general x1, matrix products, body(): jnp.dot(row_piece.reshape(piece_rows * 2, -1), out_flat, preferred_elemen...  13.6 us
    all_to_all x1, blocking collectives, body(): lax.all_to_all(attended, 'gy', split_axis=2, concat_axis=0, tiled=True)  8.34 us
    all_gather x1, blocking collectives, body(): row_piece = lax.all_gather(regrouped, 'gx', axis=0, tiled=True)  6.5 us
    all_to_all x1, waiting for transfers between devices, body(): pieces = lax.all_to_all(partial_value, 'gx', split_axis=0, concat_axis=0)  6.23 us
    all_to_all x1, waiting for transfers between devices, body(): lax.all_to_all(ready, 'gy', split_axis=0, concat_axis=2, tiled=True)  6.15 us
    all_to_all x1, starting transfers between devices, body(): lax.all_to_all(ready, 'gy', split_axis=0, concat_axis=2, tiled=True)  5.54 us
  transfers between devices with their start and end apart: 3, of which 3 were waited for; matrix products, arithmetic and copies ran while one was open for 3% of the time, Pallas kernels for 0%

profile of v1, /device:TPU:0, one launch (start us, length us, event | category | flops | bytes accessed | tf_op | source)
XLA Modules:
  0.0 115.7 jit_solution(347196364319385065)
XLA Ops:
  0.0 1.2 %reshape.116.tokens_ref = bf16[64,4096]{1,0:T(8,128)(2,1)S(1)} reshape(bf16[32,2,4096]{2,1,0:T(2,128)(2,1)} %param.7) | data formatting | bytes 1048576 | tf_op jit(solution)/shard_map/reshape | solution.py:191
  1.2 0.7 reshape.117.gain_ref
  2.0 0.0 copy-start.2
  2.0 32.1 %shard_map.73 = bf16[128,2432]{1,0:T(8,128)(2,1)} custom-call(bf16[64,4096]{1,0:T(8,128)(2,1)S(1)} %reshape.116.tokens_ref, bf16[1,4096]{1,0:T(2,128)(2,1)S(1)} %reshape.117.gain_ref, bf16[4096,18,2,128]{3,2,1,0:T(2,128)(2,1)} %bitcast.68), custom_call_target="tpu_custom_call" | custom-call | tf_op jit(solution)/shard_map/pallas_call | solution.py:177
  34.1 4.3 %all-to-all-start = ((bf16[4,32,2432]{2,1,0:T(8,128)(2,1)}), bf16[4,32,2432]{2,1,0:T(8,128)(2,1)S(1)}, u32[]{:S(2)}, u32[]{:S(2)}) async-start(bf16[4,32,2432]{2,1,0:T(8,128)(2,1)} %bitcast.1), calls=%async_computation | async-start | bytes 1245184 | tf_op jit(solution)/shard_map/all_to_all | solution.py:210
  38.4 0.0 copy-done.2
  38.4 0.1 dynamic_slice.7
  38.5 0.1 add_convert_fusion.2
  38.5 0.2 multiply_cosine_fusion
  38.8 3.2 %fusion.21 = (bf16[2,384,1,8,128]{4,3,2,1,0:T(8,128)(2,1)}, bf16[2,384,1,8,128]{4,3,2,1,0:T(8,128)(2,1)S(1)}) fusion(bf16[2,384,2,8,128]{4,3,2,1,0:T(8,128)(2,1)} %param.11), kind=kLoop, calls=%fused_computation.49 | loop fusion | bytes 6291456 | tf_op jit(solution)/shard_map/slice | solution.py:68
  42.0 6.2 %all-to-all-done = bf16[4,32,2432]{2,1,0:T(8,128)(2,1)S(1)} async-done(((bf16[4,32,2432]{2,1,0:T(8,128)(2,1)}), bf16[4,32,2432]{2,1,0:T(8,128)(2,1)S(1)}, u32[]{:S(2)}, u32[]{:S(2)}) %all-to-all-start) | async-done | bytes 622624 | tf_op jit(solution)/shard_map/all_to_all | solution.py:210
  48.2 0.1 convert_reduce_fusion
  48.4 0.0 copy-start.1
  48.4 0.1 fusion.22
  48.5 0.1 copy.72
  48.6 0.1 copy.73
  48.7 0.1 copy.50
  48.8 0.1 fusion.11
  48.9 0.2 subtract_convert_fusion
  49.0 0.1 subtract_convert_fusion.1
  49.2 0.1 pad_maximum_fusion
  49.3 0.8 copy.51
  50.1 5.5 %all-to-all-start.1 = ((bf16[8,2,2,18,128]{4,2,3,1,0:T(2,128)(2,1)}), bf16[8,2,2,18,128]{4,2,3,1,0:T(2,128)(2,1)S(1)}, u32[]{:S(2)}, u32[]{:S(2)}) async-start(bf16[8,2,2,18,128]{4,2,3,1,0:T(2,128)(2,1)} %copy.51), calls=%async_computation.1 | async-start | bytes 294912 | tf_op jit(solution)/shard_map/all_to_all | solution.py:233
  55.7 0.0 copy-done.1
  55.7 0.1 iota_compare_fusion
  55.7 6.2 %all-to-all-done.1 = bf16[8,2,2,18,128]{4,2,3,1,0:T(2,128)(2,1)S(1)} async-done(((bf16[8,2,2,18,128]{4,2,3,1,0:T(2,128)(2,1)}), bf16[8,2,2,18,128]{4,2,3,1,0:T(2,128)(2,1)S(1)}, u32[]{:S(2)}, u32[]{:S(2)}) %all-to-all-start.1) | async-done | bytes 147488 | tf_op jit(solution)/shard_map/all_to_all | solution.py:233
  62.0 0.8 fusion.24
  62.8 0.0 copy-start
  62.8 0.4 fusion.25
  63.2 0.1 fusion.16
  63.3 0.3 fusion.10
  63.7 0.2 convolution_bitcast_fusion
  63.9 0.3 copy-done
  64.2 0.5 fusion.7
  64.7 8.3 %all_to_all.46 = bf16[2,2,8,16,128]{4,3,1,0,2:T(8,128)(2,1)S(1)} all-to-all(bf16[2,2,8,16,128]{4,3,1,0,2:T(8,128)(2,1)S(1)} %copy.60), channel_id=1, replica_groups=mesh['groups'=2,'gx'=4,'gy'=4] {'gy'}, dimensions={2} | all-to-all | bytes 262144 | tf_op jit(solution)/shard_map/all_to_all | solution.py:238
  73.1 6.5 %all_gather.3 = bf16[32,2,2,16,128]{4,3,2,1,0:T(8,128)(2,1)S(1)} all-gather(bf16[8,2,2,16,128]{4,3,2,1,0:T(8,128)(2,1)S(1)} %bitcast.73), channel_id=1, replica_groups=mesh['groups'=2,'gx'=4,'gy'=4] {'gx'}, dimensions={0}, use_global_device_ids=true | all-gather | bytes 655360 | tf_op jit(solution)/shard_map/all_gather | solution.py:240
  79.6 0.2 reshape.120
  79.8 13.6 %convolution_convert_fusion = bf16[64,4096]{1,0:T(8,128)(2,1)S(1)} fusion(bf16[64,4096]{1,0:T(8,128)(2,1)S(1)} %reshape.120, bf16[4096,4096]{1,0:T(8,128)(2,1)} %bitcast.67), kind=kOutput, calls=%fused_computation | convolution fusion | flops 2147745792 | bytes 34603008 | tf_op jit(solution)/shard_map/dot_general | solution.py:242
  93.5 1.1 reshape.122
  94.6 3.5 %all-to-all-start.3 = ((bf16[4,8,2,4096]{3,2,1,0:T(2,128)(2,1)}), bf16[4,8,2,4096]{3,2,1,0:T(2,128)(2,1)S(1)}, u32[]{:S(2)}, u32[]{:S(2)}) async-start(bf16[4,8,2,4096]{3,2,1,0:T(2,128)(2,1)} %reshape.122), calls=%async_computation.3 | async-start | bytes 1048576 | tf_op jit(solution)/shard_map/all_to_all | solution.py:246
  98.1 15.2 %all-to-all-done.3 = bf16[4,8,2,4096]{3,2,1,0:T(2,128)(2,1)S(1)} async-done(((bf16[4,8,2,4096]{3,2,1,0:T(2,128)(2,1)}), bf16[4,8,2,4096]{3,2,1,0:T(2,128)(2,1)S(1)}, u32[]{:S(2)}, u32[]{:S(2)}) %all-to-all-start.3) | async-done | bytes 524320 | tf_op jit(solution)/shard_map/all_to_all | solution.py:246
  113.3 0.6 convert_reduce_fusion.1
  113.9 1.8 %convert_add_fusion = f32[8,2,4096]{2,1,0:T(2,128)} fusion(f32[8,2,4096]{2,1,0:T(2,128)S(1)} %convert_reduce_fusion.1, bf16[32,2,4096]{2,1,0:T(2,128)(2,1)} %param.7, s32[]{:T(128)S(6)} %select_n.17), kind=kLoop, calls=%fused_computation.26 | loop fusion | flops 131072 | bytes 655364 | tf_op jit(solution)/shard_map/add | solution.py:252
  (13 shorter events, 0.2 us)
Async XLA Ops:
  2.0 36.4 %copy-start.2 = (s32[32]{0:T(128)S(1)}, s32[32]{0:T(128)}, u32[]{:S(2)}) copy-start(s32[32]{0:T(128)} %param.13) | copy-start | bytes 388
  34.1 14.1 %all-to-all-start = ((bf16[4,32,2432]{2,1,0:T(8,128)(2,1)}), bf16[4,32,2432]{2,1,0:T(8,128)(2,1)S(1)}, u32[]{:S(2)}, u32[]{:S(2)}) async-start(bf16[4,32,2432]{2,1,0:T(8,128)(2,1)} %bitcast.1), calls=%async_computation | async-start | bytes 1245184 | tf_op jit(solution)/shard_map/all_to_all | solution.py:210
  48.4 7.3 %copy-start.1 = (s32[2]{0:T(128)S(1)}, s32[2]{0:T(128)}, u32[]{:S(2)}) copy-start(s32[2]{0:T(128)} %param.12) | copy-start | bytes 28
  50.1 11.8 %all-to-all-start.1 = ((bf16[8,2,2,18,128]{4,2,3,1,0:T(2,128)(2,1)}), bf16[8,2,2,18,128]{4,2,3,1,0:T(2,128)(2,1)S(1)}, u32[]{:S(2)}, u32[]{:S(2)}) async-start(bf16[8,2,2,18,128]{4,2,3,1,0:T(2,128)(2,1)} %copy.51), calls=%async_computation.1 | async-start | bytes 294912 | tf_op jit(solution)/shard_map/all_to_all | solution.py:233
  62.8 1.4 %copy-start = (bf16[2,384,1,8,128]{4,3,2,1,0:T(8,128)(2,1)S(1)}, bf16[2,384,1,8,128]{4,3,2,1,0:T(8,128)(2,1)}, u32[]{:S(2)}) copy-start(bf16[2,384,1,8,128]{4,3,2,1,0:T(8,128)(2,1)} %get-tuple-element.5) | copy-start | bytes 4718596
  94.6 18.7 %all-to-all-start.3 = ((bf16[4,8,2,4096]{3,2,1,0:T(2,128)(2,1)}), bf16[4,8,2,4096]{3,2,1,0:T(2,128)(2,1)S(1)}, u32[]{:S(2)}, u32[]{:S(2)}) async-start(bf16[4,8,2,4096]{3,2,1,0:T(2,128)(2,1)} %reshape.122), calls=%async_computation.3 | async-start | bytes 1048576 | tf_op jit(solution)/shard_map/all_to_all | solution.py:246

commit v2 on v0

--- a/solution.py
+++ b/solution.py
@@ -1,8 +1,11 @@
+import functools
 import math
 
 import jax
 import jax.numpy as jnp
 from jax import lax
+from jax.experimental import pallas as pl
+from jax.experimental.pallas import tpu as pltpu
 from jax.sharding import PartitionSpec as P
 
 D = 16384
@@ -70,6 +73,136 @@
     return attended.astype(jnp.bfloat16)
 
 
+def bring(weight_ref, chunk_ref, sems, first):
+    copies = [
+        pltpu.make_async_copy(weight_ref.at[:, first + at], chunk_ref.at[at], sems.at[at])
+        for at in range(chunk_ref.shape[0])
+    ]
+    for copy in copies:
+        copy.start()
+    return copies
+
+
+def open_kernel(block_rows, depth, tokens_ref, gain_ref, weight_ref, left_ref, extra_ref, chunk_ref, sems):
+    groups = 2
+    total_tokens, local_width = tokens_ref.shape
+    copies = bring(weight_ref, chunk_ref, sems, 0)
+    feature = lax.broadcasted_iota(jnp.int32, (128, 256), 0)
+    target = lax.broadcasted_iota(jnp.int32, (128, 256), 1)
+    spreads = [
+        jnp.where(target == feature * groups + group, 1.0, 0.0).astype(jnp.bfloat16)
+        for group in range(groups)
+    ]
+
+    def order(pieces):
+        return jnp.concatenate(
+            [
+                pieces[group][row : row + block_rows]
+                for row in range(0, total_tokens, block_rows)
+                for group in range(groups)
+            ],
+            axis=0,
+        )
+
+    def step(at, squares):
+        start = pl.multiple_of(at * depth, depth)
+        wide = tokens_ref[:, pl.ds(start, depth)].astype(jnp.float32)
+        hidden = (wide * gain_ref[:, pl.ds(start, depth)].astype(jnp.float32)).astype(jnp.bfloat16)
+        for near in range(0, depth, 128):
+            squares += wide[:, near : near + 128] * wide[:, near : near + 128]
+            spread = [
+                jnp.dot(
+                    hidden[:, near : near + 128], spreads[group], preferred_element_type=jnp.float32
+                ).astype(jnp.bfloat16)
+                for group in range(groups)
+            ]
+            begin = pl.multiple_of((start + near) * groups, 256)
+            left_ref[:, pl.ds(begin, 256)] = order(spread)
+        return squares
+
+    squares = lax.fori_loop(
+        0, local_width // depth, step, jnp.zeros((total_tokens, 128), jnp.float32)
+    )
+    summed = jnp.sum(squares, axis=1, keepdims=True)
+    coarse = summed.astype(jnp.bfloat16).astype(jnp.float32)
+    lane = lax.broadcasted_iota(jnp.int32, (total_tokens, 128), 1)
+    extra = jnp.where(lane < 64, coarse, summed - coarse)
+    extra_ref[...] = order([extra, extra]).astype(jnp.bfloat16)
+    for copy in copies:
+        copy.wait()
+
+
+def multiply_kernel(following, left_ref, chunk_ref, weight_ref, out_ref, *rest):
+    copies = []
+    if following is not None:
+        next_ref, total, sems = rest
+        copies = bring(weight_ref, next_ref, sems, following)
+    else:
+        (total,) = rest
+    count, contraction, head_dim = chunk_ref.shape
+    total[...] = jnp.zeros_like(total)
+
+    @pl.loop(0, contraction // 1024)
+    def _(step):
+        span = pl.ds(pl.multiple_of(step * 1024, 1024), 1024)
+        left = left_ref[:, span]
+        for column in range(0, count, 2):
+            right = jnp.concatenate([chunk_ref[column, span], chunk_ref[column + 1, span]], axis=1)
+            total[:, column * head_dim : (column + 2) * head_dim] += jnp.dot(
+                left, right, preferred_element_type=jnp.float32
+            )
+
+    out_ref[...] = total[...].astype(jnp.bfloat16)
+    for copy in copies:
+        copy.wait()
+
+
+def project(tokens, norm_gain, qkv_weight, places):
+    total_rows, pair, local_width = tokens.shape
+    groups, columns, head_dim = qkv_weight.shape[1:]
+    total_tokens = total_rows * pair
+    count = columns // 3
+    view = jnp.transpose(qkv_weight, (0, 2, 1, 3))
+    vmem = pl.BlockSpec(memory_space=pltpu.VMEM)
+    hbm = pl.BlockSpec(memory_space=pl.ANY)
+    chunk_shape = jax.ShapeDtypeStruct((count, local_width, groups, head_dim), jnp.bfloat16)
+    rows = total_tokens * groups
+    params = pltpu.CompilerParams(vmem_limit_bytes=14 << 20)
+    left, extra, chunk = pl.pallas_call(
+        functools.partial(open_kernel, total_tokens // places, 512),
+        out_shape=(
+            jax.ShapeDtypeStruct((rows, local_width * groups), jnp.bfloat16),
+            jax.ShapeDtypeStruct((rows, head_dim), jnp.bfloat16),
+            chunk_shape,
+        ),
+        in_specs=[vmem, vmem, hbm],
+        out_specs=(vmem, vmem, vmem),
+        scratch_shapes=[pltpu.SemaphoreType.DMA((count,))],
+        compiler_params=params,
+    )(tokens.reshape(total_tokens, local_width), norm_gain.reshape(1, local_width), view)
+    results = []
+    for following in (count, 2 * count, None):
+        last = following is None
+        out_shape = [jax.ShapeDtypeStruct((rows, count * head_dim), jnp.bfloat16)]
+        scratch = [pltpu.VMEM((rows, count * head_dim), jnp.float32)]
+        if not last:
+            out_shape.append(chunk_shape)
+            scratch.append(pltpu.SemaphoreType.DMA((count,)))
+        flat = chunk.reshape(count, local_width * groups, head_dim)
+        got = pl.pallas_call(
+            functools.partial(multiply_kernel, following),
+            out_shape=out_shape,
+            in_specs=[vmem, vmem, hbm],
+            out_specs=[vmem] * len(out_shape),
+            scratch_shapes=scratch,
+            compiler_params=params,
+        )(left, flat, view)
+        results.append(got[0])
+        if not last:
+            chunk = got[1]
+    return jnp.concatenate(results + [extra], axis=1)
+
+
 def body(tokens, norm_gain, qkv_weight, out_weight, kv_cache, lengths, positions):
     rows_local = kv_cache.shape[0]
     head_devices = lax.axis_size("gy")
@@ -81,20 +214,30 @@
     group_width = qkv_weight.shape[2]
     head_dim = qkv_weight.shape[3]
     group_size = group_width - 2
-    tokens_wide = tokens.astype(jnp.float32)
-    hidden = (tokens_wide * norm_gain.astype(jnp.float32)).astype(jnp.bfloat16)
-    squares = jnp.sum(tokens_wide * tokens_wide, axis=-1)
     block_rows = rows_local * head_devices
-    partial_value = jnp.dot(
-        hidden.reshape(total_rows * 2, local_width),
-        qkv_weight.reshape(local_width, -1),
-        preferred_element_type=jnp.float32,
-    )
-    partial_value = partial_value.reshape(total_rows, 2, groups_local, group_width, head_dim)
-    block_sum, block_squares = (
-        lax.psum_scatter(partial_value, "gx", scatter_dimension=0, tiled=True),
-        lax.psum_scatter(squares, "gx", scatter_dimension=0, tiled=True),
-    )
+    places = lax.axis_size("gx")
+    if groups_local == 2 and group_width % 6 == 0 and local_width % 512 == 0:
+        partial_value = project(tokens, norm_gain, qkv_weight, places)
+        partial_value = partial_value.reshape(places, groups_local * block_rows * 2, -1)
+        pieces = lax.all_to_all(partial_value, "gx", split_axis=0, concat_axis=0)
+        summed = jnp.sum(pieces.astype(jnp.float32), axis=0)
+        summed = summed.reshape(groups_local, block_rows, 2, group_width + 1, head_dim)
+        block_squares = summed[0, :, :, group_width, 0] + summed[0, :, :, group_width, 64]
+        block_sum = jnp.transpose(summed[:, :, :, :group_width], (1, 2, 0, 3, 4))
+    else:
+        tokens_wide = tokens.astype(jnp.float32)
+        hidden = (tokens_wide * norm_gain.astype(jnp.float32)).astype(jnp.bfloat16)
+        squares = jnp.sum(tokens_wide * tokens_wide, axis=-1)
+        partial_value = jnp.dot(
+            hidden.reshape(total_rows * 2, local_width),
+            qkv_weight.reshape(local_width, -1),
+            preferred_element_type=jnp.float32,
+        )
+        partial_value = partial_value.reshape(total_rows, 2, groups_local, group_width, head_dim)
+        block_sum, block_squares = (
+            lax.psum_scatter(partial_value, "gx", scatter_dimension=0, tiled=True),
+            lax.psum_scatter(squares, "gx", scatter_dimension=0, tiled=True),
+        )
     inv_rms = lax.rsqrt(block_squares / D + norm_eps)
     ready = finish(
         block_sum * inv_rms[:, :, None, None, None], positions, width_index * block_rows, block_rows
@@ -111,8 +254,9 @@
     product = jnp.dot(
         row_piece.reshape(piece_rows * 2, -1), out_flat, preferred_element_type=jnp.float32
     )
-    terms = product.reshape(piece_rows, 2, local_width)
-    own_sum = lax.psum_scatter(terms, "gy", scatter_dimension=0, tiled=True)
+    terms = product.astype(jnp.bfloat16).reshape(head_devices, -1, 2, local_width)
+    arrived = lax.all_to_all(terms, "gy", split_axis=0, concat_axis=0)
+    own_sum = jnp.sum(arrived.astype(jnp.float32), axis=0)
     row_share = total_rows // head_devices
     residual = lax.dynamic_slice_in_dim(tokens, head_index * row_share, row_share, 0).astype(
         jnp.float32

time: 228 us -> 102 us (0.45); the launches traced: 225 us -> 102 us
  local copies, waits for them, and re-layouts: 97 us -> 7.99 us
  waiting for transfers between devices: 47.6 us -> 27.6 us
  matrix products: 34.1 us -> 15.6 us
  Pallas kernels: 0 us -> 17.5 us
  between operations: 14.2 us -> 0.25 us
  starting transfers between devices: 4.61 us -> 13.3 us
  blocking collectives: 23.3 us -> 14.8 us
    unnamed x12 -> x8, local copies, waits for them, and re-layouts: 91.7 us -> 0.2 us
    reduce_scatter x2 -> x0, waiting for transfers between devices: 41.4 us -> none  [the longest x1 25.1 us: body(): own_sum = lax.psum_scatter(terms, 'gy', scatter_dimension=0, tiled=True)]
    all_to_all x0 -> x2, waiting for transfers between devices: none -> 21.5 us  [the longest x1 15.2 us: body(): arrived = lax.all_to_all(terms, 'gy', split_axis=0, concat_axis=0)]
    dot_general x1 -> x0, matrix products: 17.5 us -> none  [body(): jnp.dot(hidden.reshape(total_rows * 2, local_width), qkv_weight.reshape(l...]
    pallas_call x0 -> x4, Pallas kernels: none -> 17.5 us  [the longest x3 12.7 us: project(): pl.pallas_call(functools.partial(multiply_kernel, following), out_shape=o...]
    unnamed x1 -> x0, blocking collectives: 8.37 us -> none
    all_to_all x0 -> x2, starting transfers between devices: none -> 7.73 us  [the longest x1 4.26 us: body(): pieces = lax.all_to_all(partial_value, 'gx', split_axis=0, concat_axis=0)]
    reshape x0 -> x5, local copies, waits for them, and re-layouts: none -> 3.35 us  [the longest x1 1.24 us: project(): tokens.reshape(total_tokens, local_width)]
  transfers between devices with their start and end apart: 3 -> 3, of which waited for: 3 -> 3; matrix products, arithmetic and copies ran while one was open for 2% -> 4% of each run, Pallas kernels for 0% -> 0%
where the time goes in v2:
time: 102 us
  waiting for transfers between devices  27.6 us (27%)
  Pallas kernels  17.5 us (17%)
  matrix products  15.6 us (15%)
  blocking collectives  14.8 us (15%)
  starting transfers between devices  13.3 us (13%)
  local copies, waits for them, and re-layouts  7.99 us (8%)
  other arithmetic  4.58 us (4%)
    all_to_all x1, waiting for transfers between devices, body(): arrived = lax.all_to_all(terms, 'gy', split_axis=0, concat_axis=0)  15.2 us
    dot_general x1, matrix products, body(): jnp.dot(row_piece.reshape(piece_rows * 2, -1), out_flat, preferred_elemen...  13.6 us
    pallas_call x3, Pallas kernels, project(): pl.pallas_call(functools.partial(multiply_kernel, following), out_shape=o...  12.7 us
    all_to_all x1, blocking collectives, body(): lax.all_to_all(attended, 'gy', split_axis=2, concat_axis=0, tiled=True)  8.34 us
    all_gather x1, blocking collectives, body(): row_piece = lax.all_gather(regrouped, 'gx', axis=0, tiled=True)  6.5 us
    all_to_all x1, waiting for transfers between devices, body(): pieces = lax.all_to_all(partial_value, 'gx', split_axis=0, concat_axis=0)  6.22 us
    all_to_all x1, waiting for transfers between devices, body(): lax.all_to_all(ready, 'gy', split_axis=0, concat_axis=2, tiled=True)  6.15 us
    all_to_all x1, starting transfers between devices, body(): lax.all_to_all(ready, 'gy', split_axis=0, concat_axis=2, tiled=True)  5.53 us
  transfers between devices with their start and end apart: 3, of which 3 were waited for; matrix products, arithmetic and copies ran while one was open for 4% of the time, Pallas kernels for 0%

profile of v2, /device:TPU:0, one launch (start us, length us, event | category | flops | bytes accessed | tf_op | source)
XLA Modules:
  0.0 101.6 jit_solution(7988507802875561067)
XLA Ops:
  0.0 1.2 %reshape.125.tokens_ref = bf16[64,4096]{1,0:T(8,128)(2,1)S(1)} reshape(bf16[32,2,4096]{2,1,0:T(2,128)(2,1)} %param.7) | data formatting | bytes 1048576 | tf_op jit(solution)/shard_map/reshape | solution.py:182
  1.2 0.7 reshape.126.gain_ref
  2.0 4.8 %shard_map.73 = (bf16[128,8192]{1,0:T(8,128)(2,1)S(1)}, bf16[128,128]{1,0:T(8,128)(2,1)S(1)}, bf16[6,4096,2,128]{3,2,1,0:T(2,128)(2,1)S(1)}) custom-call(bf16[64,4096]{1,0:T(8,128)(2,1)S(1)} %reshape.125.tokens_ref, bf16[1,4096]{1,0:T(2,128)(2,1)S(1)} %reshape.126.gain_ref, bf16[4096,18,2,128]{3,2,1,0:T(2,128)(2,1)} %bitcast.73), custom_call_target="tpu_custom_call" | custom-call | tf_op jit(solution)/shard_map/pallas_call | solution.py:171
  6.8 4.8 %shard_map.74 = (bf16[128,768]{1,0:T(8,128)(2,1)S(1)}, bf16[6,4096,2,128]{3,2,1,0:T(2,128)(2,1)S(1)}) custom-call(bf16[128,8192]{1,0:T(8,128)(2,1)S(1)} %get-tuple-element.12.left_ref, bf16[6,8192,128]{2,1,0:T(8,128)(2,1)S(1)} %bitcast.70, bf16[4096,18,2,128]{3,2,1,0:T(2,128)(2,1)} %bitcast.74), custom_call_target="tpu_custom_call" | custom-call | tf_op jit(solution)/shard_map/pallas_call | solution.py:192
  11.6 4.8 %shard_map.75 = (bf16[128,768]{1,0:T(8,128)(2,1)S(1)}, bf16[6,4096,2,128]{3,2,1,0:T(2,128)(2,1)S(1)}) custom-call(bf16[128,8192]{1,0:T(8,128)(2,1)S(1)} %get-tuple-element.12.left_ref, bf16[6,8192,128]{2,1,0:T(8,128)(2,1)S(1)} %bitcast.71, bf16[4096,18,2,128]{3,2,1,0:T(2,128)(2,1)} %bitcast.75), custom_call_target="tpu_custom_call" | custom-call | tf_op jit(solution)/shard_map/pallas_call | solution.py:192
  16.4 3.1 %shard_map.76 = bf16[128,768]{1,0:T(8,128)(2,1)S(1)} custom-call(bf16[128,8192]{1,0:T(8,128)(2,1)S(1)} %get-tuple-element.12.left_ref, bf16[6,8192,128]{2,1,0:T(8,128)(2,1)S(1)} %bitcast.72, bf16[4096,18,2,128]{3,2,1,0:T(2,128)(2,1)} %bitcast.76), custom_call_target="tpu_custom_call" | custom-call | tf_op jit(solution)/shard_map/pallas_call | solution.py:192
  19.5 0.0 copy-start.2
  19.5 0.9 pad_maximum_fusion
  20.4 4.3 %all-to-all-start = ((bf16[4,32,2432]{2,1,0:T(8,128)(2,1)}), bf16[4,32,2432]{2,1,0:T(8,128)(2,1)S(1)}, u32[]{:S(2)}, u32[]{:S(2)}) async-start(bf16[4,32,2432]{2,1,0:T(8,128)(2,1)} %bitcast.4), calls=%async_computation | async-start | bytes 1245184 | tf_op jit(solution)/shard_map/all_to_all | solution.py:222
  24.6 0.0 copy-done.2
  24.6 0.1 dynamic_slice.7
  24.7 0.1 add_convert_fusion.2
  24.8 0.2 multiply_cosine_fusion
  25.0 3.3 %fusion.21 = (bf16[2,384,1,8,128]{4,3,2,1,0:T(8,128)(2,1)}, bf16[2,384,1,8,128]{4,3,2,1,0:T(8,128)(2,1)S(1)}) fusion(bf16[2,384,2,8,128]{4,3,2,1,0:T(8,128)(2,1)} %param.11), kind=kLoop, calls=%fused_computation.50 | loop fusion | bytes 6291456 | tf_op jit(solution)/shard_map/slice | solution.py:68
  28.3 6.2 %all-to-all-done = bf16[4,32,2432]{2,1,0:T(8,128)(2,1)S(1)} async-done(((bf16[4,32,2432]{2,1,0:T(8,128)(2,1)}), bf16[4,32,2432]{2,1,0:T(8,128)(2,1)S(1)}, u32[]{:S(2)}, u32[]{:S(2)}) %all-to-all-start) | async-done | bytes 622624 | tf_op jit(solution)/shard_map/all_to_all | solution.py:222
  34.5 0.1 convert_reduce_fusion
  34.6 0.0 copy-start.1
  34.6 0.1 fusion.22
  34.7 0.1 copy.72
  34.8 0.1 copy.73
  34.9 0.1 copy.50
  35.0 0.1 fusion.11
  35.1 0.1 subtract_convert_fusion.1
  35.3 0.2 subtract_convert_fusion
  35.4 0.1 pad_maximum_fusion.1
  35.6 0.8 copy.51
  36.4 5.5 %all-to-all-start.1 = ((bf16[8,2,2,18,128]{4,2,3,1,0:T(2,128)(2,1)}), bf16[8,2,2,18,128]{4,2,3,1,0:T(2,128)(2,1)S(1)}, u32[]{:S(2)}, u32[]{:S(2)}) async-start(bf16[8,2,2,18,128]{4,2,3,1,0:T(2,128)(2,1)} %copy.51), calls=%async_computation.1 | async-start | bytes 294912 | tf_op jit(solution)/shard_map/all_to_all | solution.py:245
  41.9 0.0 copy-done.1
  41.9 0.1 iota_compare_fusion
  42.0 6.2 %all-to-all-done.1 = bf16[8,2,2,18,128]{4,2,3,1,0:T(2,128)(2,1)S(1)} async-done(((bf16[8,2,2,18,128]{4,2,3,1,0:T(2,128)(2,1)}), bf16[8,2,2,18,128]{4,2,3,1,0:T(2,128)(2,1)S(1)}, u32[]{:S(2)}, u32[]{:S(2)}) %all-to-all-start.1) | async-done | bytes 147488 | tf_op jit(solution)/shard_map/all_to_all | solution.py:245
  48.3 0.4 fusion.25
  48.7 0.0 copy-start
  48.7 0.8 fusion.24
  49.5 0.3 fusion.10
  49.8 0.1 fusion.16
  49.9 0.2 convolution_bitcast_fusion
  50.2 0.0 copy-done
  50.2 0.5 fusion.7
  50.7 8.3 %all_to_all.46 = bf16[2,2,8,16,128]{4,3,1,0,2:T(8,128)(2,1)S(1)} all-to-all(bf16[2,2,8,16,128]{4,3,1,0,2:T(8,128)(2,1)S(1)} %copy.60), channel_id=1, replica_groups=mesh['groups'=2,'gx'=4,'gy'=4] {'gy'}, dimensions={2} | all-to-all | bytes 262144 | tf_op jit(solution)/shard_map/all_to_all | solution.py:250
  59.1 6.5 %all_gather.3 = bf16[32,2,2,16,128]{4,3,2,1,0:T(8,128)(2,1)S(1)} all-gather(bf16[8,2,2,16,128]{4,3,2,1,0:T(8,128)(2,1)S(1)} %bitcast.82), channel_id=1, replica_groups=mesh['groups'=2,'gx'=4,'gy'=4] {'gx'}, dimensions={0}, use_global_device_ids=true | all-gather | bytes 655360 | tf_op jit(solution)/shard_map/all_gather | solution.py:252
  65.6 0.2 reshape.132
  65.8 13.6 %convolution_convert_fusion = bf16[64,4096]{1,0:T(8,128)(2,1)S(1)} fusion(bf16[64,4096]{1,0:T(8,128)(2,1)S(1)} %reshape.132, bf16[4096,4096]{1,0:T(8,128)(2,1)} %bitcast.77), kind=kOutput, calls=%fused_computation | convolution fusion | flops 2147745792 | bytes 34603008 | tf_op jit(solution)/shard_map/dot_general | solution.py:254
  79.5 1.1 %reshape.134 = bf16[4,8,2,4096]{3,2,1,0:T(2,128)(2,1)} reshape(bf16[64,4096]{1,0:T(8,128)(2,1)S(1)} %convolution_convert_fusion) | data formatting | bytes 1048576 | tf_op jit(solution)/shard_map/reshape | solution.py:257
  80.6 3.5 %all-to-all-start.3 = ((bf16[4,8,2,4096]{3,2,1,0:T(2,128)(2,1)}), bf16[4,8,2,4096]{3,2,1,0:T(2,128)(2,1)S(1)}, u32[]{:S(2)}, u32[]{:S(2)}) async-start(bf16[4,8,2,4096]{3,2,1,0:T(2,128)(2,1)} %reshape.134), calls=%async_computation.3 | async-start | bytes 1048576 | tf_op jit(solution)/shard_map/all_to_all | solution.py:258
  84.1 15.2 %all-to-all-done.3 = bf16[4,8,2,4096]{3,2,1,0:T(2,128)(2,1)S(1)} async-done(((bf16[4,8,2,4096]{3,2,1,0:T(2,128)(2,1)}), bf16[4,8,2,4096]{3,2,1,0:T(2,128)(2,1)S(1)}, u32[]{:S(2)}, u32[]{:S(2)}) %all-to-all-start.3) | async-done | bytes 524320 | tf_op jit(solution)/shard_map/all_to_all | solution.py:258
  99.3 0.6 convert_reduce_fusion.1
  99.9 1.8 %convert_add_fusion = f32[8,2,4096]{2,1,0:T(2,128)} fusion(f32[8,2,4096]{2,1,0:T(2,128)S(1)} %convert_reduce_fusion.1, bf16[32,2,4096]{2,1,0:T(2,128)(2,1)} %param.7, s32[]{:T(128)S(6)} %select_n.17), kind=kLoop, calls=%fused_computation.27 | loop fusion | flops 131072 | bytes 655364 | tf_op jit(solution)/shard_map/add | solution.py:264
  (13 shorter events, 0.2 us)
Async XLA Ops:
  19.5 5.2 %copy-start.2 = (s32[32]{0:T(128)S(1)}, s32[32]{0:T(128)}, u32[]{:S(2)}) copy-start(s32[32]{0:T(128)} %param.13) | copy-start | bytes 388
  20.4 14.1 %all-to-all-start = ((bf16[4,32,2432]{2,1,0:T(8,128)(2,1)}), bf16[4,32,2432]{2,1,0:T(8,128)(2,1)S(1)}, u32[]{:S(2)}, u32[]{:S(2)}) async-start(bf16[4,32,2432]{2,1,0:T(8,128)(2,1)} %bitcast.4), calls=%async_computation | async-start | bytes 1245184 | tf_op jit(solution)/shard_map/all_to_all | solution.py:222
  34.6 7.3 %copy-start.1 = (s32[2]{0:T(128)S(1)}, s32[2]{0:T(128)}, u32[]{:S(2)}) copy-start(s32[2]{0:T(128)} %param.12) | copy-start | bytes 28
  36.4 11.8 %all-to-all-start.1 = ((bf16[8,2,2,18,128]{4,2,3,1,0:T(2,128)(2,1)}), bf16[8,2,2,18,128]{4,2,3,1,0:T(2,128)(2,1)S(1)}, u32[]{:S(2)}, u32[]{:S(2)}) async-start(bf16[8,2,2,18,128]{4,2,3,1,0:T(2,128)(2,1)} %copy.51), calls=%async_computation.1 | async-start | bytes 294912 | tf_op jit(solution)/shard_map/all_to_all | solution.py:245
  48.7 1.5 %copy-start = (bf16[2,384,1,8,128]{4,3,2,1,0:T(8,128)(2,1)S(1)}, bf16[2,384,1,8,128]{4,3,2,1,0:T(8,128)(2,1)}, u32[]{:S(2)}) copy-start(bf16[2,384,1,8,128]{4,3,2,1,0:T(8,128)(2,1)} %get-tuple-element.19) | copy-start | bytes 4718596
  80.6 18.7 %all-to-all-start.3 = ((bf16[4,8,2,4096]{3,2,1,0:T(2,128)(2,1)}), bf16[4,8,2,4096]{3,2,1,0:T(2,128)(2,1)S(1)}, u32[]{:S(2)}, u32[]{:S(2)}) async-start(bf16[4,8,2,4096]{3,2,1,0:T(2,128)(2,1)} %reshape.134), calls=%async_computation.3 | async-start | bytes 1048576 | tf_op jit(solution)/shard_map/all_to_all | solution.py:258
